TPU v7x, 256 devices: a whole 4x4x8 slice. The times are simulated.
256 devices in a mesh: seq: 64 (over y, z, core), tp: 4 (over x).
Axes of the slice: x: 4, y: 4, z: 8, core: 2. Of those that a mesh axis runs over, the one named last changes fastest.
Arguments:
- inputs: bfloat16 [4, 4, 1024], P(None, None, 'tp'), may hold values from -64 to 64
- attention_gain: bfloat16 [1024], replicated, may hold values from 0.099609375 to 1.8984375
- forward_gain: bfloat16 [1024], replicated, may hold values from 0.099609375 to 1.8984375
- query_weight: bfloat16 [1024, 1024], P(None, 'tp'), may hold values from -0.1875 to 0.1875
- key_weight: bfloat16 [1024, 1024], P(None, 'tp'), may hold values from -0.1875 to 0.1875
- value_weight: bfloat16 [1024, 1024], P(None, 'tp'), may hold values from -0.1875 to 0.1875
- output_weight: bfloat16 [1024, 1024], P('tp'), may hold values from -0.1875 to 0.1875
- gate_weight: bfloat16 [1024, 4096], P(None, 'tp'), may hold values from -0.1875 to 0.1875
- up_weight: bfloat16 [1024, 4096], P(None, 'tp'), may hold values from -0.1875 to 0.1875
- down_weight: bfloat16 [4096, 1024], P('tp'), may hold values from -0.09375 to 0.09375
- variate_bias: float32 [2, 16], replicated, may hold values from -256 to 256
- cache_keys: bfloat16 [4, 32768, 1024], P(None, 'seq', 'tp'), may hold values from -15 to 15
- cache_values: bfloat16 [4, 32768, 1024], P(None, 'seq', 'tp'), may hold values from -12 to 12
- cache_variates: int32 [4, 32768], P(None, 'seq'), may hold values from 0 to 7
- cache_mask: int32 [4, 32768], P(None, 'seq'), may hold values 0 or 1
- cache_lengths: int32 [4], replicated, may hold values from 1 to 32768, as said below
- fresh_flags: int32 [4], replicated, may hold values 0 or 1
- new_variates: int32 [4, 4], replicated, may hold values from 0 to 7
- new_times: int32 [4, 4], replicated, may hold values from 0 to 32771
Outputs:
- hidden_states: bfloat16 [4, 4, 1024], P(None, None, 'tp')
- new_keys: bfloat16 [4, 4, 1024], P(None, None, 'tp')
- new_values: bfloat16 [4, 4, 1024], P(None, None, 'tp')
Inputs may be any that keep to these rules, and one draw needn't show every extreme that they name: `cache_lengths`: some request has exactly 32768 filled positions.
All inputs are finite; a program needn't handle non-finite values. No bound on the sum of `cache_mask` on one device may be relied on, other than what follows from the above.
Results may differ from a plain program's by a relative error of at most 0.014.
Values may be sent and summed in bfloat16 or wider, within the bound.
A program may use at most 64 MiB of HBM per device.

v0:
```python
import math

import jax
import jax.numpy as jnp
from jax import lax
from jax.sharding import PartitionSpec as P

D = 1024
HEAD_DIM = 64
STEPS = 4


epsilon = 1e-05


def rotated(blocks, times):
    half = blocks.shape[-1] // 2
    ladder = jnp.arange(half, dtype=jnp.float32) * (2.0 / blocks.shape[-1])
    inverse = jnp.exp(-math.log(10000.0) * ladder)
    angles = times.astype(jnp.float32)[:, None] * inverse[None, :]
    cosine = jnp.cos(angles)[:, None, :]
    sine = jnp.sin(angles)[:, None, :]
    first = blocks[..., :half]
    second = blocks[..., half:]
    return jnp.concatenate(
        [first * cosine - second * sine, second * cosine + first * sine], axis=-1
    )


def join_parts(earlier, later):
    peak = jnp.maximum(earlier[0], later[0])
    factor_one = jnp.exp(earlier[0] - peak)
    factor_two = jnp.exp(later[0] - peak)
    totals = earlier[1] * factor_one + later[1] * factor_two
    repeat_by = earlier[2].shape[-1] // earlier[0].shape[-1]
    sums = earlier[2] * jnp.repeat(factor_one, repeat_by, axis=1) + later[2] * jnp.repeat(
        factor_two, repeat_by, axis=1
    )
    return (peak, totals, sums)


def on_device(
    inputs,
    attention_gain,
    forward_gain,
    query_weight,
    key_weight,
    value_weight,
    output_weight,
    gate_weight,
    up_weight,
    down_weight,
    variate_bias,
    cache_keys,
    cache_values,
    cache_variates,
    cache_mask,
    cache_lengths,
    fresh_flags,
    new_variates,
    new_times,
):
    local_width = query_weight.shape[1]
    local_heads = local_width // HEAD_DIM
    requests = inputs.shape[0]
    columns = inputs.shape[2]
    span = cache_keys.shape[1]
    scale = 1.0 / math.sqrt(HEAD_DIM)
    column_start = lax.axis_index("tp") * columns
    head_start = lax.axis_index("tp") * local_heads
    bias_local = lax.dynamic_slice_in_dim(variate_bias, head_start, local_heads, 1)
    same_bias = bias_local[0]
    other_bias = bias_local[1]
    positions = lax.axis_index("seq") * span + jnp.arange(span, dtype=jnp.int32)
    usable = (
        (positions[None, :] < cache_lengths[:, None])
        & (cache_mask == 1)
        & (fresh_flags[:, None] == 0)
    )
    key_blocks = cache_keys.reshape(requests, span, local_heads, HEAD_DIM)
    value_blocks = cache_values.reshape(requests, span, local_heads, HEAD_DIM)
    gain_first = attention_gain.astype(jnp.float32)[None, :]
    gain_second = forward_gain.astype(jnp.float32)[None, :]
    gain_first_local = lax.dynamic_slice_in_dim(gain_first, column_start, columns, 1)
    gain_second_local = lax.dynamic_slice_in_dim(gain_second, column_start, columns, 1)
    hidden_list = []
    key_list = []
    value_list = []
    for step_index in range(STEPS):
        current_low = inputs[:, step_index, :]
        current_local = current_low.astype(jnp.float32)
        square_sum = lax.psum(jnp.sum(current_local * current_local, axis=1), "tp")
        inverse_rms = lax.rsqrt(square_sum / D + epsilon)
        normed_local = (current_local * inverse_rms[:, None] * gain_first_local).astype(
            jnp.bfloat16
        )
        normed = lax.all_gather(normed_local, "tp", axis=1, tiled=True)
        query_full = jnp.dot(normed, query_weight, preferred_element_type=jnp.float32)
        key_full = jnp.dot(normed, key_weight, preferred_element_type=jnp.float32)
        value_full = jnp.dot(normed, value_weight, preferred_element_type=jnp.float32)
        times_now = new_times[:, step_index]
        queries_now = rotated(
            query_full.reshape(requests, local_heads, HEAD_DIM), times_now
        ).astype(jnp.bfloat16)
        keys_now = rotated(key_full.reshape(requests, local_heads, HEAD_DIM), times_now).astype(
            jnp.bfloat16
        )
        values_now = value_full.reshape(requests, local_heads, HEAD_DIM).astype(jnp.bfloat16)
        key_list.append(keys_now)
        value_list.append(values_now)
        variate_now = new_variates[:, step_index]
        same_cache = cache_variates == variate_now[:, None]
        scores = (
            jnp.einsum("rhe,rche->rhc", queries_now, key_blocks, preferred_element_type=jnp.float32)
            * scale
        )
        scores = scores + jnp.where(
            same_cache[:, None, :], same_bias[None, :, None], other_bias[None, :, None]
        )
        scores = jnp.where(usable[:, None, :], scores, -1e30)
        local_peak = jnp.max(scores, axis=2)
        raw = jnp.where(usable[:, None, :], jnp.exp(scores - local_peak[:, :, None]), 0.0)
        local_total = jnp.sum(raw, axis=2)
        local_sum = jnp.einsum(
            "rhc,rche->rhe",
            raw.astype(jnp.bfloat16),
            value_blocks,
            preferred_element_type=jnp.float32,
        ).reshape(requests, local_width)
        peak_all = lax.pmax(local_peak, "seq")
        factor = jnp.exp(local_peak - peak_all)
        totals_all, sums_all = lax.psum(
            (local_total * factor, local_sum * jnp.repeat(factor, HEAD_DIM, axis=1)), "seq"
        )
        merged = (peak_all, totals_all, sums_all)
        fresh_keys = jnp.stack(key_list, axis=1)
        fresh_values = jnp.stack(value_list, axis=1)
        same_new = new_variates[:, : step_index + 1] == variate_now[:, None]
        new_scores = (
            jnp.einsum("rhe,rshe->rhs", queries_now, fresh_keys, preferred_element_type=jnp.float32)
            * scale
        )
        new_scores = new_scores + jnp.where(
            same_new[:, None, :], same_bias[None, :, None], other_bias[None, :, None]
        )
        new_peak = jnp.max(new_scores, axis=2)
        new_raw = jnp.exp(new_scores - new_peak[:, :, None])
        new_total = jnp.sum(new_raw, axis=2)
        new_sum = jnp.einsum(
            "rhs,rshe->rhe",
            new_raw.astype(jnp.bfloat16),
            fresh_values,
            preferred_element_type=jnp.float32,
        ).reshape(requests, local_width)
        joined = join_parts(merged, (new_peak, new_total, new_sum))
        attention = (joined[2] / jnp.repeat(joined[1], HEAD_DIM, axis=1)).astype(jnp.bfloat16)
        partial_out = jnp.dot(attention, output_weight, preferred_element_type=jnp.float32)
        projected_local = lax.psum_scatter(partial_out, "tp", scatter_dimension=1, tiled=True)
        middle_local = (current_local + projected_local).astype(jnp.bfloat16).astype(jnp.float32)
        middle_sum = lax.psum(jnp.sum(middle_local * middle_local, axis=1), "tp")
        second_rms = lax.rsqrt(middle_sum / D + epsilon)
        normed_two_local = (middle_local * second_rms[:, None] * gain_second_local).astype(
            jnp.bfloat16
        )
        normed_two = lax.all_gather(normed_two_local, "tp", axis=1, tiled=True)
        gate_part = jnp.dot(normed_two, gate_weight, preferred_element_type=jnp.float32)
        up_part = jnp.dot(normed_two, up_weight, preferred_element_type=jnp.float32)
        activated = (jax.nn.silu(gate_part) * up_part).astype(jnp.bfloat16)
        down_part = jnp.dot(activated, down_weight, preferred_element_type=jnp.float32)
        forward = lax.psum_scatter(down_part, "tp", scatter_dimension=1, tiled=True)
        hidden_list.append((middle_local + forward).astype(jnp.bfloat16))
    hidden_states = jnp.stack(hidden_list, axis=1)
    new_keys = jnp.stack(key_list, axis=1).reshape(requests, STEPS, local_width)
    new_values = jnp.stack(value_list, axis=1).reshape(requests, STEPS, local_width)
    return (hidden_states, new_keys, new_values)


def solution(mesh):
    return jax.shard_map(
        on_device,
        mesh=mesh,
        in_specs=(
            P(None, None, "tp"),
            P(),
            P(),
            P(None, "tp"),
            P(None, "tp"),
            P(None, "tp"),
            P("tp", None),
            P(None, "tp"),
            P(None, "tp"),
            P("tp", None),
            P(),
            P(None, "seq", "tp"),
            P(None, "seq", "tp"),
            P(None, "seq"),
            P(None, "seq"),
            P(),
            P(),
            P(),
            P(),
        ),
        out_specs=(P(None, None, "tp"), P(None, None, "tp"), P(None, None, "tp")),
        check_vma=False,
    )
```

profile of v0, /device:TPU:1, one launch (start us, length us, event | category | flops | bytes accessed | tf_op | source)
XLA Modules:
  0.0 711.7 jit_solution(17226373592038998446)
XLA Ops:
  7.3 0.9 fusion.172
  8.7 9.3 %all-reduce.3 = (f32[4]{0:T(128)S(1)}, f32[4]{0:T(128)S(1)}, f32[4]{0:T(128)S(1)}, f32[4]{0:T(128)S(1)}) all-reduce(f32[4]{0:T(128)S(1)} %fusion.94, f32[4]{0:T(128)S(1)} %fusion.106, f32[4]{0:T(128)S(1)} %fusion.102, f32[4]{0:T(128)S(1)} %fusion.98), channel_id=1, replica_groups=mesh['seq'=64,'tp'=4] {'tp'}, use_global_device_ids=true, to_apply=%region_1.0 | all-reduce | flops 16 | bytes 128 | tf_op jit(solution)/shard_map/psum | solution.py:92
  18.0 0.8 dynamic-slice.6
  18.9 8.1 %all_gather.24 = bf16[4,1024]{1,0:T(4,128)(2,1)S(1)} all-gather(bf16[4,256]{1,0:T(4,128)(2,1)S(1)} %get-tuple-element.136), channel_id=1, replica_groups=mesh['seq'=64,'tp'=4] {'tp'}, dimensions={1}, use_global_device_ids=true | all-gather | bytes 10240 | tf_op jit(solution)/shard_map/all_gather | solution.py:97
  27.0 1.2 convolution_convert_fusion.3
  28.2 1.2 fusion.174
  29.4 8.1 %all_gather.26 = bf16[4,1024]{1,0:T(4,128)(2,1)S(1)} all-gather(bf16[4,256]{1,0:T(4,128)(2,1)S(1)} %get-tuple-element.137), channel_id=1, replica_groups=mesh['seq'=64,'tp'=4] {'tp'}, dimensions={1}, use_global_device_ids=true | all-gather | bytes 10240 | tf_op jit(solution)/shard_map/all_gather | solution.py:97
  37.5 1.2 convolution_convert_fusion.2
  38.7 1.2 fusion.177
  40.3 8.1 %all_gather.28 = bf16[4,1024]{1,0:T(4,128)(2,1)S(1)} all-gather(bf16[4,256]{1,0:T(4,128)(2,1)S(1)} %get-tuple-element.138), channel_id=1, replica_groups=mesh['seq'=64,'tp'=4] {'tp'}, dimensions={1}, use_global_device_ids=true | all-gather | bytes 10240 | tf_op jit(solution)/shard_map/all_gather | solution.py:97
  49.0 8.1 %all_gather.30 = bf16[4,1024]{1,0:T(4,128)(2,1)S(1)} all-gather(bf16[4,256]{1,0:T(4,128)(2,1)S(1)} %get-tuple-element.139), channel_id=1, replica_groups=mesh['seq'=64,'tp'=4] {'tp'}, dimensions={1}, use_global_device_ids=true | all-gather | bytes 10240 | tf_op jit(solution)/shard_map/all_gather | solution.py:97
  60.0 1.5 copy.47
  63.3 1.5 copy.48
  65.3 140.8 %all-reduce.1 = (f32[4,4]{1,0:T(4,128)S(1)}, f32[4,4]{1,0:T(4,128)S(1)}, f32[4,4]{1,0:T(4,128)S(1)}, f32[4,4]{1,0:T(4,128)S(1)}) all-reduce(f32[4,4]{1,0:T(4,128)S(1)} %get-tuple-element.78, f32[4,4]{1,0:T(4,128)S(1)} %get-tuple-element.125, f32[4,4]{1,0:T(4,128)S(1)} %get-tuple-element.123, ...), channel_id=1, replica_groups=mesh['seq'=64,'tp'=4] {'seq'}, use_global_device_ids=true, to_apply=%region_40.41 | all-reduce | flops 64 | bytes 512 | tf_op jit(solution)/shard_map/pmax | solution.py:130
  206.7 1.7 fusion.14
  208.4 1.6 fusion.16
  211.6 241.0 %all-reduce = (f32[4,4]{1,0:T(4,128)S(1)}, f32[4,256]{1,0:T(4,128)S(1)}, f32[4,4]{1,0:T(4,128)S(1)}, f32[4,256]{1,0:T(4,128)S(1)}, f32[4,4]{1,0:T(4,128)S(1)}, /...) all-reduce(f32[4,4]{1,0:T(4,128)S(1)} %get-tuple-element.70, ...), channel_id=1, replica_groups=mesh['seq'=64,'tp'=4] {'seq'}, use_global_device_ids=true, to_apply=%region_44.45 | all-reduce | flops 4160 | bytes 33280 | tf_op jit(solution)/shard_map/psum | solution.py:132
  453.1 1.2 convolution_bitcast_fusion.4
  455.8 1.2 convolution_bitcast_fusion.5
  458.5 1.2 convolution_bitcast_fusion.6
  460.4 1.2 convolution_bitcast_fusion.7
  462.1 0.6 copy.56
  463.3 11.4 %reduce-scatter.37.cloned.1.call-done = f32[256,4]{1,0:T(8,128)} async-done(((f32[1024,4]{1,0:T(8,128)}), f32[256,4]{1,0:T(8,128)}) %reduce-scatter.37.cloned.1.call-update) | async-done | bytes 4112
  474.8 1.0 copy.105
  475.7 25.3 %reduce-scatter.33.cloned.1.call-done = f32[256,4]{1,0:T(8,128)} async-done(((f32[1024,4]{1,0:T(8,128)}), f32[256,4]{1,0:T(8,128)}) %reduce-scatter.33.cloned.1.call-update) | async-done | bytes 4112
  501.0 1.0 copy.101
  502.0 25.3 %reduce-scatter.29.cloned.1.call-done = f32[256,4]{1,0:T(8,128)} async-done(((f32[1024,4]{1,0:T(8,128)}), f32[256,4]{1,0:T(8,128)}) %reduce-scatter.29.cloned.1.call-update) | async-done | bytes 4112
  527.3 1.0 copy.97
  528.3 25.2 %reduce-scatter.25.cloned.1.call-done = f32[256,4]{1,0:T(8,128)} async-done(((f32[1024,4]{1,0:T(8,128)}), f32[256,4]{1,0:T(8,128)}) %reduce-scatter.25.cloned.1.call-update) | async-done | bytes 4112
  553.5 1.0 copy.93
  554.7 6.6 all-reduce.2
  561.4 8.1 %all_gather.25 = bf16[4,1024]{1,0:T(4,128)(2,1)S(1)} all-gather(bf16[4,256]{1,0:T(4,128)(2,1)S(1)} %get-tuple-element.130), channel_id=1, replica_groups=mesh['seq'=64,'tp'=4] {'tp'}, dimensions={1}, use_global_device_ids=true | all-gather | bytes 10240 | tf_op jit(solution)/shard_map/all_gather | solution.py:165
  569.5 8.1 %all_gather.27 = bf16[4,1024]{1,0:T(4,128)(2,1)S(1)} all-gather(bf16[4,256]{1,0:T(4,128)(2,1)S(1)} %get-tuple-element.131), channel_id=1, replica_groups=mesh['seq'=64,'tp'=4] {'tp'}, dimensions={1}, use_global_device_ids=true | all-gather | bytes 10240 | tf_op jit(solution)/shard_map/all_gather | solution.py:165
  577.6 8.1 %all_gather.29 = bf16[4,1024]{1,0:T(4,128)(2,1)S(1)} all-gather(bf16[4,256]{1,0:T(4,128)(2,1)S(1)} %get-tuple-element.132), channel_id=1, replica_groups=mesh['seq'=64,'tp'=4] {'tp'}, dimensions={1}, use_global_device_ids=true | all-gather | bytes 10240 | tf_op jit(solution)/shard_map/all_gather | solution.py:165
  586.8 4.1 convolution_bitcast_fusion.3
  591.1 4.1 convolution_bitcast_fusion.2
  595.2 4.1 convolution_bitcast_fusion.1
  599.3 8.1 %all_gather.31 = bf16[4,1024]{1,0:T(4,128)(2,1)S(1)} all-gather(bf16[4,256]{1,0:T(4,128)(2,1)S(1)} %get-tuple-element.133), channel_id=1, replica_groups=mesh['seq'=64,'tp'=4] {'tp'}, dimensions={1}, use_global_device_ids=true | all-gather | bytes 10240 | tf_op jit(solution)/shard_map/all_gather | solution.py:165
  608.2 4.1 convolution_bitcast_fusion
  612.3 12.3 %reduce-scatter.27.cloned.1.call-done = f32[256,4]{1,0:T(8,128)} async-done(((f32[1024,4]{1,0:T(8,128)}), f32[256,4]{1,0:T(8,128)}) %reduce-scatter.27.cloned.1.call-update) | async-done | bytes 4112
  624.5 1.0 copy.95
  625.5 25.2 %reduce-scatter.31.cloned.1.call-done = f32[256,4]{1,0:T(8,128)} async-done(((f32[1024,4]{1,0:T(8,128)}), f32[256,4]{1,0:T(8,128)}) %reduce-scatter.31.cloned.1.call-update) | async-done | bytes 4112
  650.7 1.0 copy.99
  651.7 25.3 %reduce-scatter.35.cloned.1.call-done = f32[256,4]{1,0:T(8,128)} async-done(((f32[1024,4]{1,0:T(8,128)}), f32[256,4]{1,0:T(8,128)}) %reduce-scatter.35.cloned.1.call-update) | async-done | bytes 4112
  677.0 1.0 copy.103
  678.0 25.3 %reduce-scatter.39.cloned.1.call-done = f32[256,4]{1,0:T(8,128)} async-done(((f32[1024,4]{1,0:T(8,128)}), f32[256,4]{1,0:T(8,128)}) %reduce-scatter.39.cloned.1.call-update) | async-done | bytes 4112
  703.3 1.0 copy.107
  704.3 0.6 copy.54
  (202 shorter events, 16.8 us)
Async XLA Ops:
  7.2 578.5 %copy-start = (bf16[1024,1024]{1,0:T(8,128)(2,1)S(1)}, bf16[1024,1024]{1,0:T(8,128)(2,1)}, u32[]{:S(2)}) copy-start(bf16[1024,1024]{1,0:T(8,128)(2,1)} %param.26) | copy-start | bytes 6291460
  7.2 41.2 %copy-start.1 = (bf16[1024,256]{1,0:T(8,128)(2,1)S(1)}, bf16[1024,256]{1,0:T(8,128)(2,1)}, u32[]{:S(2)}) copy-start(bf16[1024,256]{1,0:T(8,128)(2,1)} %param.24) | copy-start | bytes 1572868
  7.2 41.4 %copy-start.2 = (bf16[1024,256]{1,0:T(8,128)(2,1)S(1)}, bf16[1024,256]{1,0:T(8,128)(2,1)}, u32[]{:S(2)}) copy-start(bf16[1024,256]{1,0:T(8,128)(2,1)} %param.23) | copy-start | bytes 1572868
  7.2 467.6 %reduce-scatter.37.cloned.1.call-start = ((), (), s32[]{:S(2)}) async-start(), calls=%async_computation.14 | async-start | bytes 655360
  18.0 21.9 %copy-start.3 = (bf16[1024,256]{1,0:T(8,128)(2,1)S(1)}, bf16[1024,256]{1,0:T(8,128)(2,1)}, u32[]{:S(2)}) copy-start(bf16[1024,256]{1,0:T(8,128)(2,1)} %param.22) | copy-start | bytes 1572868
  39.9 17.7 %copy-start.11 = (f32[2,16]{1,0:T(2,128)S(1)}, f32[2,16]{1,0:T(2,128)}, u32[]{:S(2)}) copy-start(f32[2,16]{1,0:T(2,128)} %param.29) | copy-start | bytes 388
  39.9 17.7 %copy-start.14 = (s32[4]{0:T(128)S(1)}, s32[4]{0:T(128)}, u32[]{:S(2)}) copy-start(s32[4]{0:T(128)} %param.35) | copy-start | bytes 52
  40.0 17.8 %copy-start.8 = (s32[4,4]{1,0:T(4,128)S(1)}, s32[4,4]{1,0:T(4,128)}, u32[]{:S(2)}) copy-start(s32[4,4]{1,0:T(4,128)} %param.37) | copy-start | bytes 196
  40.0 18.0 %copy-start.7 = (s32[4,4]{1,0:T(4,128)S(1)}, s32[4,4]{1,0:T(4,128)}, u32[]{:S(2)}) copy-start(s32[4,4]{1,0:T(4,128)} %param.36) | copy-start | bytes 196
  62.8 2.1 copy-start.10
  62.8 2.1 copy-start.13
  62.8 2.2 copy-start.9
  64.9 141.4 %copy-start.5 = (bf16[4,512,256]{1,2,0:T(8,128)(2,1)}, bf16[4,512,256]{1,2,0:T(8,128)(2,1)S(1)}, u32[]{:S(2)}) copy-start(bf16[4,512,256]{1,2,0:T(8,128)(2,1)S(1)} %copy.48) | copy-start | bytes 3145732
  206.7 3.3 copy-start.6
  206.7 246.4 %copy-start.4 = (bf16[256,1024]{1,0:T(8,128)(2,1)S(1)}, bf16[256,1024]{1,0:T(8,128)(2,1)}, u32[]{:S(2)}) copy-start(bf16[256,1024]{1,0:T(8,128)(2,1)} %param.25) | copy-start | bytes 1572868
  454.3 46.7 %reduce-scatter.33.cloned.1.call-start = ((), (), s32[]{:S(2)}) async-start(), calls=%async_computation.12 | async-start | bytes 655360
  457.0 5.1 copy-start.12
  457.0 70.3 %reduce-scatter.29.cloned.1.call-start = ((), (), s32[]{:S(2)}) async-start(), calls=%async_computation.10 | async-start | bytes 655360
  459.7 93.8 %reduce-scatter.25.cloned.1.call-start = ((), (), s32[]{:S(2)}) async-start(), calls=%async_computation.8 | async-start | bytes 655360
  461.6 162.9 %reduce-scatter.27.cloned.1.call-start = ((), (), s32[]{:S(2)}) async-start(), calls=%async_computation.9 | async-start | bytes 655360
  590.9 59.8 %reduce-scatter.31.cloned.1.call-start = ((), (), s32[]{:S(2)}) async-start(), calls=%async_computation.11 | async-start | bytes 655360
  607.4 69.6 %reduce-scatter.35.cloned.1.call-start = ((), (), s32[]{:S(2)}) async-start(), calls=%async_computation.13 | async-start | bytes 655360
  608.1 95.1 %reduce-scatter.39.cloned.1.call-start = ((), (), s32[]{:S(2)}) async-start(), calls=%async_computation.15 | async-start | bytes 655360
Sparse Core Ops, SparseCore 0:
  454.4 20.2 reduce-scatter.36
  477.3 23.6 reduce-scatter.32
  503.6 23.7 reduce-scatter.28
  529.7 23.7 reduce-scatter.24
  591.0 33.4 reduce-scatter.26
  626.9 23.7 reduce-scatter.30
  653.2 23.7 reduce-scatter.34
  679.5 23.7 reduce-scatter.38
where the time goes:
time: 713 us; the launch traced here: 712 us
  blocking collectives  462 us (65%)
  waiting for transfers between devices  176 us (25%)
  matrix products  34.7 us (5%)
  local copies, waits for them, and re-layouts  18.9 us (3%)
  between operations  14.5 us (2%)
    psum x1, blocking collectives, on_device(): lax.psum((local_total * factor, local_sum * jnp.repeat(factor, HEAD_DIM,...  241 us
    unnamed x16, waiting for transfers between devices  176 us
    pmax x1, blocking collectives, on_device(): peak_all = lax.pmax(local_peak, 'seq')  141 us
    all_gather x4, blocking collectives, on_device(): normed = lax.all_gather(normed_local, 'tp', axis=1, tiled=True)  32.3 us
    all_gather x4, blocking collectives, on_device(): normed_two = lax.all_gather(normed_two_local, 'tp', axis=1, tiled=True)  32.3 us
    unnamed x8, matrix products  21 us
  transfers between devices with their start and end apart: 8, of which 8 were waited for; matrix products, arithmetic and copies ran while one was open for 4% of the time, Pallas kernels for 0%

commit v1 on v0

v1 whole, which is shorter than its diff:
```python
import math

import numpy as np

import jax
import jax.numpy as jnp
from jax import lax
from jax.experimental import pallas as pl
from jax.experimental.pallas import tpu as pltpu
from jax.sharding import PartitionSpec as P

D = 1024
HEAD_DIM = 64
STEPS = 4
REQ = 4
TOK = REQ * STEPS
TP = 4
LW = 256
LH = 4
SPAN = 512
NB = 8
NZ = 8
EPS = 1e-05
SCALE = 1.0 / math.sqrt(HEAD_DIM)
NEG = -1e30

MESH = pl.DeviceIdType.MESH
F32 = jnp.float32
BF16 = jnp.bfloat16


def iota(shape, axis):
    return lax.broadcasted_iota(jnp.int32, shape, axis)


def dot(a, b):
    return jnp.dot(a, b, preferred_element_type=F32)


def dot_t(a, b):
    return lax.dot_general(a, b, (((1,), (1,)), ((), ())), preferred_element_type=F32)


def merge(parts):
    peaks = [part[:, 96:97] for part in parts]
    peak = peaks[0]
    for other in peaks[1:]:
        peak = jnp.maximum(peak, other)
    joined = jnp.exp(peaks[0] - peak) * parts[0]
    for part, own in zip(parts[1:], peaks[1:]):
        joined = joined + jnp.exp(own - peak) * part
    return joined, peak


def kernel(
    x_hbm, again_hbm, fgain_hbm, wq_hbm, wk_hbm, wv_hbm, wo_hbm, wg_hbm, wu_hbm, wd_hbm,
    bias_hbm, ck_hbm, cv_hbm, cvar_hbm, cmask_hbm, clen_hbm, fresh_hbm, nvar_hbm, ntime_hbm,
    inv_hbm,
    hid_out, nk_out, nv_out,
    xg, again, fgain, wq, wk, wv, wo, wg, wu, wd,
    bias, ck, cv, cvar, cmask, clen, fresh, nvar, ntime, inv,
    xf, xb, sbuf, rslots, nbuf, zslots, cslots, midall, midf, midc, dbuf, dslots,
    hid_v, nk_v, nv_v,
    lsem, osem, ssem, rsem,
):
    s = lax.axis_index("seq")
    i = lax.axis_index("tp")
    y = s // 16
    z = lax.rem(s // 2, NZ)
    c = lax.rem(s, 2)
    b = y * 2 + c

    def tp_peer(d):
        return (s, lax.rem(i + d, TP))

    def b_peer(d):
        other = lax.rem(b + d, NB)
        return other, ((other // 2) * 16 + z * 2 + lax.rem(other, 2), i)

    def z_peer(d):
        return (y * 16 + lax.rem(z + d, NZ) * 2 + c, i)

    barrier = pltpu.get_barrier_semaphore()
    for d in range(1, TP):
        pl.semaphore_signal(barrier, inc=1, device_id=tp_peer(d), device_id_type=MESH)
    for d in range(1, NB):
        pl.semaphore_signal(barrier, inc=1, device_id=b_peer(d)[1], device_id_type=MESH)
    for d in range(1, NZ):
        pl.semaphore_signal(barrier, inc=1, device_id=z_peer(d), device_id_type=MESH)

    count = [0]

    def fetch(src, dst):
        copy = pltpu.make_async_copy(src, dst, lsem.at[count[0]])
        count[0] += 1
        copy.start()
        return copy

    x_copy = fetch(x_hbm, xg.at[i])
    time_copy = fetch(ntime_hbm, ntime)
    inv_copy = fetch(inv_hbm, inv)
    small = [
        fetch(nvar_hbm, nvar), fetch(bias_hbm, bias), fetch(clen_hbm, clen),
        fetch(fresh_hbm, fresh), fetch(cvar_hbm, cvar), fetch(cmask_hbm, cmask),
        fetch(again_hbm, again), fetch(fgain_hbm, fgain),
    ]
    qkv_copies = [fetch(wq_hbm, wq), fetch(wk_hbm, wk), fetch(wv_hbm, wv)]
    k_copies = [fetch(ck_hbm.at[r], ck.at[r]) for r in range(REQ)]
    v_copies = [fetch(cv_hbm.at[r], cv.at[r]) for r in range(REQ)]
    wo_copy = fetch(wo_hbm, wo)
    wg_copy = fetch(wg_hbm, wg)
    wu_copy = fetch(wu_hbm, wu)
    wd_copy = fetch(wd_hbm, wd)

    sends = []

    def send(src, dst, phase, peer):
        copy = pltpu.make_async_remote_copy(
            src_ref=src, dst_ref=dst, send_sem=ssem.at[len(sends)], recv_sem=rsem.at[phase],
            device_id=peer, device_id_type=MESH,
        )
        copy.start()
        sends.append(copy)

    def arrived(region, phase):
        pltpu.make_async_copy(region, region, rsem.at[phase]).wait()

    x_copy.wait()
    pl.semaphore_wait(barrier, TP - 1 + NB - 1 + NZ - 1)
    for d in range(1, TP):
        send(xg.at[i], xg.at[i], 0, tp_peer(d))

    time_copy.wait()
    inv_copy.wait()
    for copy in small:
        copy.wait()
    lane = iota((TOK, 128), 1)
    row16 = iota((TOK, 128), 0)
    times = jnp.zeros((TOK, 128), F32)
    for n in range(TOK):
        times = jnp.where(row16 == n, ntime[n // STEPS, n % STEPS].astype(F32), times)
    angles = times * inv[...]
    cosine = jnp.cos(angles)
    sine = jnp.sin(angles)
    sine = jnp.where((lane & 32) == 0, -sine, sine)
    cosine = jnp.concatenate([cosine, cosine], axis=1)
    sine = jnp.concatenate([sine, sine], axis=1)

    rowh = iota((16, 1), 0)
    same_col = jnp.zeros((16, 1), F32)
    other_col = jnp.zeros((16, 1), F32)
    for h in range(LH):
        same_col = jnp.where((rowh & 3) == h, bias[0, i * LH + h], same_col)
        other_col = jnp.where((rowh & 3) == h, bias[1, i * LH + h], other_col)
    position = s * SPAN + iota((1, SPAN), 1)
    usable = []
    biases = []
    for r in range(REQ):
        ok = (
            (position < clen[r])
            & (cmask[r:r + 1, :] == 1)
            & ((iota((1, SPAN), 1) * 0 + fresh[r]) == 0)
        )
        usable.append(jnp.where(ok, 1, 0))
        var_col = jnp.zeros((16, 1), jnp.int32)
        for t in range(STEPS):
            var_col = jnp.where((rowh >> 2) == t, nvar[r, t], var_col)
        biases.append(jnp.where(cvar[r:r + 1, :] == var_col, same_col, other_col))

    arrived(xg.at[0:TP - 1], 0)
    for r in range(REQ):
        for j in range(TP):
            slab = xg[j, r].astype(F32)
            xf[STEPS * r:STEPS * r + STEPS, LW * j:LW * j + LW] = slab
            xb[2 * r, :, LW * j:LW * j + LW] = slab[0:2, :]
            xb[2 * r + 1, :, LW * j:LW * j + LW] = slab[2:4, :]

    def norm(values, gain_ref):
        square = jnp.sum(values * values, axis=1, keepdims=True)
        gain = gain_ref[...].astype(F32).reshape(1, D)
        return (values * lax.rsqrt(square / D + EPS) * gain).astype(BF16)

    normed = norm(xf[...], again)
    for copy in qkv_copies:
        copy.wait()
    lane2 = iota((TOK, LW), 1)

    def rope(values):
        swapped = jnp.where(
            (lane2 & 32) == 0, pltpu.roll(values, LW - 32, 1), pltpu.roll(values, 32, 1)
        )
        return (values * cosine + swapped * sine).astype(BF16)

    queries = rope(dot(normed, wq[...]))
    keys = rope(dot(normed, wk[...]))
    values = dot(normed, wv[...]).astype(BF16)

    pick = jnp.where((iota((64, TOK), 0) >> 2) == iota((64, TOK), 1), 1.0, 0.0).astype(BF16)
    spread = dot(pick, queries)
    head_lane = (iota((64, LW), 1) >> 6) == (iota((64, LW), 0) & 3)
    spread = jnp.where(head_lane, spread, 0.0).astype(BF16)

    def state(total, peak, sums, rows):
        mine = (iota((rows, LW), 1) >> 6) == (iota((rows, LW), 0) & 3)
        sums = jnp.where(mine, sums, 0.0)
        folded = sums[:, 0:128] + sums[:, 128:256]
        folded = folded + pltpu.roll(folded, 64, 1)
        at = iota((rows, 128), 1)
        return jnp.where(at < 64, folded, jnp.where(at < 96, total, peak))

    for r in range(REQ):
        k_copies[r].wait()
        scores = dot_t(spread[16 * r:16 * r + 16, :], ck[r]) * SCALE + biases[r]
        scores = jnp.where(usable[r] == 1, scores, NEG)
        peak = jnp.max(scores, axis=1, keepdims=True)
        raw = jnp.where(usable[r] == 1, jnp.exp(scores - peak), 0.0)
        total = jnp.sum(raw, axis=1, keepdims=True)
        v_copies[r].wait()
        sums = dot(raw.astype(BF16), cv[r])
        block = state(total, peak, sums, 16)
        sbuf[2 * r] = block[0:8, :]
        sbuf[2 * r + 1] = block[8:16, :]

    for d in range(1, NB):
        other, peer = b_peer(d)
        send(sbuf.at[other], rslots.at[b], 1, peer)

    keys32 = keys.astype(F32)
    values32 = values.astype(F32)
    for r in range(REQ):
        nk_v[r] = keys32[STEPS * r:STEPS * r + STEPS, :].astype(BF16)
        nv_v[r] = values32[STEPS * r:STEPS * r + STEPS, :].astype(BF16)
    nk_copy = pltpu.make_async_copy(nk_v, nk_out, osem.at[0])
    nv_copy = pltpu.make_async_copy(nv_v, nv_out, osem.at[1])
    nk_copy.start()
    nv_copy.start()
    row64 = iota((64, 1), 0)
    col16 = iota((1, TOK), 1)
    same64 = jnp.zeros((64, 1), F32)
    other64 = jnp.zeros((64, 1), F32)
    for h in range(LH):
        same64 = jnp.where((row64 & 3) == h, bias[0, i * LH + h], same64)
        other64 = jnp.where((row64 & 3) == h, bias[1, i * LH + h], other64)
    var64 = jnp.zeros((64, 1), jnp.int32)
    var16 = jnp.zeros((1, TOK), jnp.int32)
    for n in range(TOK):
        token_variate = nvar[n // STEPS, n % STEPS]
        var64 = jnp.where((row64 >> 2) == n, token_variate, var64)
        var16 = jnp.where(col16 == n, token_variate, var16)
    new_scores = dot_t(spread, keys) * SCALE + jnp.where(var64 == var16, same64, other64)
    row_token = row64 >> 2
    causal = ((col16 >> 2) == (row_token >> 2)) & ((col16 & 3) <= (row_token & 3))
    new_scores = jnp.where(causal, new_scores, NEG)
    new_peak = jnp.max(new_scores, axis=1, keepdims=True)
    new_raw = jnp.where(causal, jnp.exp(new_scores - new_peak), 0.0)
    new_total = jnp.sum(new_raw, axis=1, keepdims=True)
    new_sums = dot(new_raw.astype(BF16), values)
    new_state = state(new_total, new_peak, new_sums, 64)
    for k in range(NB):
        nbuf[k] = new_state[8 * k:8 * k + 8, :]
    rslots[b] = sbuf[b]

    arrived(rslots.at[0:NB - 1], 1)
    joined, peak = merge([rslots[k] for k in range(NB)])
    lane8 = iota((8, 128), 1)
    zslots[z] = jnp.where(lane8 < 96, joined, peak)
    for d in range(1, NZ):
        send(zslots.at[z], zslots.at[z], 2, z_peer(d))
    arrived(zslots.at[0:NZ - 1], 2)
    joined, _ = merge([zslots[k] for k in range(NZ)] + [nbuf[b]])
    attention = joined / joined[:, 64:65]
    attention = jnp.where(lane8 < 64, attention, pltpu.roll(attention, 64, 1))
    attention = jnp.concatenate([attention, attention], axis=1)
    row8 = iota((8, LW), 0)
    attention = jnp.where((iota((8, LW), 1) >> 6) == (row8 & 3), attention, 0.0)
    first = jnp.sum(jnp.where(row8 < 4, attention, 0.0), axis=0, keepdims=True)
    second = jnp.sum(jnp.where(row8 < 4, 0.0, attention), axis=0, keepdims=True)
    attention = jnp.where(row8 == 0, first, second).astype(BF16)

    wo_copy.wait()
    cslots[i] = dot(attention, wo[...])[0:2, :]
    for d in range(1, TP):
        send(cslots.at[i], cslots.at[i], 3, tp_peer(d))
    arrived(cslots.at[0:TP - 1], 3)
    middle = xb[b] + (cslots[0] + cslots[1] + cslots[2] + cslots[3])
    midall[b] = middle.astype(BF16)
    for d in range(1, NB):
        send(midall.at[b], midall.at[b], 4, b_peer(d)[1])
    arrived(midall.at[0:NB - 1], 4)
    for k in range(NB):
        midf[2 * k:2 * k + 2, :] = midall[k].astype(F32)

    middle = midf[...]
    for j in range(TP):
        midc[j] = middle[:, LW * j:LW * j + LW]
    normed_two = norm(middle, fgain)
    wg_copy.wait()
    gate = dot(normed_two, wg[...])
    wu_copy.wait()
    up = dot(normed_two, wu[...])
    activated = (gate / (1.0 + jnp.exp(-gate)) * up).astype(BF16)
    wd_copy.wait()
    down = dot(activated, wd[...])
    for j in range(TP):
        dbuf[j] = down[:, LW * j:LW * j + LW]
    for d in range(1, TP):
        send(dbuf.at[lax.rem(i + d, TP)], dslots.at[i], 5, tp_peer(d))
    dslots[i] = dbuf[i]
    arrived(dslots.at[0:TP - 1], 5)
    hidden = midc[i] + (dslots[0] + dslots[1] + dslots[2] + dslots[3])
    for r in range(REQ):
        hid_v[r] = hidden[STEPS * r:STEPS * r + STEPS, :].astype(BF16)
    hid_copy = pltpu.make_async_copy(hid_v, hid_out, osem.at[2])
    hid_copy.start()
    for copy in sends:
        copy.wait_send()
    nk_copy.wait()
    nv_copy.wait()
    hid_copy.wait()


def on_device(*args):
    inverse = np.exp(
        np.float32(-math.log(10000.0)) * (np.arange(32, dtype=np.float32) * np.float32(2.0 / 64))
    ).astype(np.float32)
    inverse = jnp.asarray(np.tile(inverse, 4)[None, :])
    vmem, smem = pltpu.VMEM, pltpu.SMEM
    out = jax.ShapeDtypeStruct((REQ, STEPS, LW), BF16)
    any_spec = pl.BlockSpec(memory_space=pl.ANY)
    return pl.pallas_call(
        kernel,
        out_shape=(out, out, out),
        in_specs=[any_spec] * 20,
        out_specs=(any_spec,) * 3,
        scratch_shapes=[
            vmem((TP, REQ, STEPS, LW), BF16),
            vmem((D,), BF16), vmem((D,), BF16),
            vmem((D, LW), BF16), vmem((D, LW), BF16), vmem((D, LW), BF16),
            vmem((LW, D), BF16),
            vmem((D, D), BF16), vmem((D, D), BF16), vmem((D, D), BF16),
            smem((2, 16), F32),
            vmem((REQ, SPAN, LW), BF16), vmem((REQ, SPAN, LW), BF16),
            vmem((REQ, SPAN), jnp.int32), vmem((REQ, SPAN), jnp.int32),
            smem((REQ,), jnp.int32), smem((REQ,), jnp.int32),
            smem((REQ, STEPS), jnp.int32), smem((REQ, STEPS), jnp.int32),
            vmem((1, 128), F32),
            vmem((TOK, D), F32),
            vmem((NB, 2, D), F32),
            vmem((NB, 8, 128), F32),
            vmem((NB, 8, 128), F32),
            vmem((NB, 8, 128), F32),
            vmem((NZ, 8, 128), F32),
            vmem((TP, 2, D), F32),
            vmem((NB, 2, D), BF16),
            vmem((TOK, D), F32),
            vmem((TP, TOK, LW), F32),
            vmem((TP, TOK, LW), F32),
            vmem((TP, TOK, LW), F32),
            vmem((REQ, STEPS, LW), BF16),
            vmem((REQ, STEPS, LW), BF16),
            vmem((REQ, STEPS, LW), BF16),
            pltpu.SemaphoreType.DMA((32,)),
            pltpu.SemaphoreType.DMA((3,)),
            pltpu.SemaphoreType.DMA((32,)),
            pltpu.SemaphoreType.DMA((6,)),
        ],
        compiler_params=pltpu.CompilerParams(
            collective_id=0, has_side_effects=True, vmem_limit_bytes=48 * 1024 * 1024
        ),
        name="layer",
    )(*args, inverse)


def solution(mesh):
    return jax.shard_map(
        on_device,
        mesh=mesh,
        in_specs=(
            P(None, None, "tp"),
            P(),
            P(),
            P(None, "tp"),
            P(None, "tp"),
            P(None, "tp"),
            P("tp", None),
            P(None, "tp"),
            P(None, "tp"),
            P("tp", None),
            P(),
            P(None, "seq", "tp"),
            P(None, "seq", "tp"),
            P(None, "seq"),
            P(None, "seq"),
            P(),
            P(),
            P(),
            P(),
        ),
        out_specs=(P(None, None, "tp"), P(None, None, "tp"), P(None, None, "tp")),
        check_vma=False,
    )
```

time: 713 us -> 53.9 us (0.08)
  blocking collectives: 462 us -> 0 us
  waiting for transfers between devices: 176 us -> 0 us
  Pallas kernels: 0 us -> 36.7 us
  matrix products: 34.7 us -> 0 us
  between operations: 14.5 us -> 0.67 us
    psum x3 -> x0, blocking collectives: 257 us -> none  [the longest x1 241 us: on_device(): lax.psum((local_total * factor, local_sum * jnp.repeat(factor, HEAD_DIM,...]
    unnamed x16 -> x0, waiting for transfers between devices: 176 us -> none
    pmax x1 -> x0, blocking collectives: 141 us -> none  [on_device(): peak_all = lax.pmax(local_peak, 'seq')]
    all_gather x8 -> x0, blocking collectives: 64.6 us -> none  [the longest x4 32.3 us: on_device(): normed = lax.all_gather(normed_local, 'tp', axis=1, tiled=True)]
    pallas_call x0 -> x1, Pallas kernels: none -> 36.7 us  [on_device(): pl.pallas_call(kernel, out_shape=(out, out, out), in_specs=[any_spec] * 2...]
    unnamed x8 -> x0, matrix products: 21 us -> none
    dot_general x30 -> x0, matrix products: 13.7 us -> none  [the longest x4 4.09 us: on_device(): jnp.einsum('rhc,rche->rhe', raw.astype(jnp.bfloat16), value_blocks, prefe...]
    unnamed x43 -> x37, local copies, waits for them, and re-layouts: 12.7 us -> 15.9 us
  transfers between devices with their start and end apart: 8 -> 0, of which waited for: 8 -> 0; matrix products, arithmetic and copies ran while one was open for 4% -> 0% of each run, Pallas kernels for 0% -> 0%
where the time goes in v1:
time: 53.9 us; the launch traced here: 53.2 us
  Pallas kernels  36.7 us (68%)
  local copies, waits for them, and re-layouts  15.9 us (29%)
  between operations  0.67 us (1%)
    pallas_call x1, Pallas kernels, on_device(): pl.pallas_call(kernel, out_shape=(out, out, out), in_specs=[any_spec] * 2...  36.7 us
    unnamed x37, local copies, waits for them, and re-layouts  15.9 us

profile of v1, /device:TPU:1, one launch (start us, length us, event | category | flops | bytes accessed | tf_op | source)
XLA Modules:
  0.0 53.2 jit_solution(16197656706061033188)
XLA Ops:
  0.6 0.0 copy-start
  0.6 1.2 %copy-done = bf16[4,512,256]{2,1,0:T(8,128)(2,1)S(1)} copy-done((bf16[4,512,256]{2,1,0:T(8,128)(2,1)S(1)}, bf16[4,512,256]{2,1,0:T(8,128)(2,1)}, u32[]{:S(2)}) %copy-start) | copy-done | bytes 1048600
  1.9 0.0 copy-start.1
  1.9 1.2 %copy-done.1 = bf16[4,512,256]{2,1,0:T(8,128)(2,1)S(1)} copy-done((bf16[4,512,256]{2,1,0:T(8,128)(2,1)S(1)}, bf16[4,512,256]{2,1,0:T(8,128)(2,1)}, u32[]{:S(2)}) %copy-start.1) | copy-done | bytes 1048600
  3.1 0.0 copy-start.2
  3.1 1.0 %copy-done.2 = bf16[1024,256]{1,0:T(8,128)(2,1)S(1)} copy-done((bf16[1024,256]{1,0:T(8,128)(2,1)S(1)}, bf16[1024,256]{1,0:T(8,128)(2,1)}, u32[]{:S(2)}) %copy-start.2) | copy-done | bytes 524312
  4.1 0.0 copy-start.3
  4.1 1.0 %copy-done.3 = bf16[1024,256]{1,0:T(8,128)(2,1)S(1)} copy-done((bf16[1024,256]{1,0:T(8,128)(2,1)S(1)}, bf16[1024,256]{1,0:T(8,128)(2,1)}, u32[]{:S(2)}) %copy-start.3) | copy-done | bytes 524312
  5.2 0.0 copy-start.4
  5.2 1.0 %copy-done.4 = bf16[1024,256]{1,0:T(8,128)(2,1)S(1)} copy-done((bf16[1024,256]{1,0:T(8,128)(2,1)S(1)}, bf16[1024,256]{1,0:T(8,128)(2,1)}, u32[]{:S(2)}) %copy-start.4) | copy-done | bytes 524312
  6.2 0.0 copy-start.5
  6.2 1.0 %copy-done.5 = bf16[256,1024]{1,0:T(8,128)(2,1)S(1)} copy-done((bf16[256,1024]{1,0:T(8,128)(2,1)S(1)}, bf16[256,1024]{1,0:T(8,128)(2,1)}, u32[]{:S(2)}) %copy-start.5) | copy-done | bytes 524312
  7.3 0.0 copy-start.6
  7.3 0.7 %copy-done.6 = bf16[4,4,256]{2,1,0:T(4,128)(2,1)S(1)} copy-done((bf16[4,4,256]{2,1,0:T(4,128)(2,1)S(1)}, bf16[4,4,256]{2,1,0:T(4,128)(2,1)}, u32[]{:S(2)}) %copy-start.6) | copy-done | bytes 8216
  8.0 0.0 copy-start.7
  8.0 0.7 %copy-done.7 = s32[4,512]{1,0:T(4,128)S(1)} copy-done((s32[4,512]{1,0:T(4,128)S(1)}, s32[4,512]{1,0:T(4,128)}, u32[]{:S(2)}) %copy-start.7) | copy-done | bytes 8216
  8.7 0.0 copy-start.8
  8.7 0.7 %copy-done.8 = s32[4,512]{1,0:T(4,128)S(1)} copy-done((s32[4,512]{1,0:T(4,128)S(1)}, s32[4,512]{1,0:T(4,128)}, u32[]{:S(2)}) %copy-start.8) | copy-done | bytes 8216
  9.4 0.0 copy-start.9
  9.4 0.7 %copy-done.9 = bf16[1024]{0:T(1024)(128)(2,1)S(1)} copy-done((bf16[1024]{0:T(1024)(128)(2,1)S(1)}, bf16[1024]{0:T(1024)(128)(2,1)}, u32[]{:S(2)}) %copy-start.9) | copy-done | bytes 2072
  10.0 0.0 copy-start.10
  10.0 0.7 %copy-done.10 = bf16[1024]{0:T(1024)(128)(2,1)S(1)} copy-done((bf16[1024]{0:T(1024)(128)(2,1)S(1)}, bf16[1024]{0:T(1024)(128)(2,1)}, u32[]{:S(2)}) %copy-start.10) | copy-done | bytes 2072
  10.7 0.0 copy-start.11
  10.7 0.7 %copy-done.11 = s32[4,4]{1,0:T(4,128)S(1)} copy-done((s32[4,4]{1,0:T(4,128)S(1)}, s32[4,4]{1,0:T(4,128)}, u32[]{:S(2)}) %copy-start.11) | copy-done | bytes 88
  11.4 0.0 copy-start.12
  11.4 0.7 %copy-done.12 = s32[4,4]{1,0:T(4,128)S(1)} copy-done((s32[4,4]{1,0:T(4,128)S(1)}, s32[4,4]{1,0:T(4,128)}, u32[]{:S(2)}) %copy-start.12) | copy-done | bytes 88
  12.1 0.0 copy-start.13
  12.1 0.7 %copy-done.13 = f32[2,16]{1,0:T(2,128)S(1)} copy-done((f32[2,16]{1,0:T(2,128)S(1)}, f32[2,16]{1,0:T(2,128)}, u32[]{:S(2)}) %copy-start.13) | copy-done | bytes 152
  12.8 0.0 copy-start.14
  12.8 0.7 %copy-done.14 = s32[4]{0:T(128)S(1)} copy-done((s32[4]{0:T(128)S(1)}, s32[4]{0:T(128)}, u32[]{:S(2)}) %copy-start.14) | copy-done | bytes 40
  13.4 0.0 copy-start.15
  13.4 0.7 %copy-done.15 = s32[4]{0:T(128)S(1)} copy-done((s32[4]{0:T(128)S(1)}, s32[4]{0:T(128)}, u32[]{:S(2)}) %copy-start.15) | copy-done | bytes 40
  14.1 0.0 copy-start.16
  14.1 0.7 %copy-done.16 = f32[1,128]{1,0:T(1,128)S(1)} copy-done((f32[1,128]{1,0:T(1,128)S(1)}, f32[1,128]{1,0:T(1,128)}, u32[]{:S(2)}) %copy-start.16) | copy-done | bytes 536
  14.7 36.7 %layer.1 = (bf16[4,4,256]{2,1,0:T(4,128)(2,1)S(1)}, bf16[4,4,256]{2,1,0:T(4,128)(2,1)S(1)}, bf16[4,4,256]{2,1,0:T(4,128)(2,1)S(1)}) custom-call(bf16[4,4,256]{2,1,0:T(4,128)(2,1)S(1)} %copy-done.6, bf16[1024]{0:T(1024)(128)(2,1)S(1)} %copy-done.9, bf16[1024]{0:T(1024)(128)(2,1)S(1)} %copy-done.10, bf16[1024,256]{1,0:T(8,128)(2,1)S(1)} %copy-done.2, ...), custom_call_target="tpu_custom_call" | custom-call | tf_op jit(solution)/shard_map/layer/pallas_call | solution.py:330
  51.5 0.6 %copy.26 = bf16[4,4,256]{2,1,0:T(4,128)(2,1)} copy(bf16[4,4,256]{2,1,0:T(4,128)(2,1)S(1)} %get-tuple-element.6) | data formatting | bytes 16384
  52.1 0.6 %copy.27 = bf16[4,4,256]{2,1,0:T(4,128)(2,1)} copy(bf16[4,4,256]{2,1,0:T(4,128)(2,1)S(1)} %get-tuple-element.7) | data formatting | bytes 16384
  52.7 0.6 %copy.28 = bf16[4,4,256]{2,1,0:T(4,128)(2,1)} copy(bf16[4,4,256]{2,1,0:T(4,128)(2,1)S(1)} %get-tuple-element.8) | data formatting | bytes 16384
Async XLA Ops:
  0.6 1.2 %copy-start = (bf16[4,512,256]{2,1,0:T(8,128)(2,1)S(1)}, bf16[4,512,256]{2,1,0:T(8,128)(2,1)}, u32[]{:S(2)}) copy-start(bf16[4,512,256]{2,1,0:T(8,128)(2,1)} %ck_hbm.1) | copy-start | bytes 3145732
  1.9 1.2 %copy-start.1 = (bf16[4,512,256]{2,1,0:T(8,128)(2,1)S(1)}, bf16[4,512,256]{2,1,0:T(8,128)(2,1)}, u32[]{:S(2)}) copy-start(bf16[4,512,256]{2,1,0:T(8,128)(2,1)} %cv_hbm.1) | copy-start | bytes 3145732
  3.1 1.0 %copy-start.2 = (bf16[1024,256]{1,0:T(8,128)(2,1)S(1)}, bf16[1024,256]{1,0:T(8,128)(2,1)}, u32[]{:S(2)}) copy-start(bf16[1024,256]{1,0:T(8,128)(2,1)} %wq_hbm.1) | copy-start | bytes 1572868
  4.1 1.0 %copy-start.3 = (bf16[1024,256]{1,0:T(8,128)(2,1)S(1)}, bf16[1024,256]{1,0:T(8,128)(2,1)}, u32[]{:S(2)}) copy-start(bf16[1024,256]{1,0:T(8,128)(2,1)} %wk_hbm.1) | copy-start | bytes 1572868
  5.2 1.0 %copy-start.4 = (bf16[1024,256]{1,0:T(8,128)(2,1)S(1)}, bf16[1024,256]{1,0:T(8,128)(2,1)}, u32[]{:S(2)}) copy-start(bf16[1024,256]{1,0:T(8,128)(2,1)} %wv_hbm.1) | copy-start | bytes 1572868
  6.2 1.0 %copy-start.5 = (bf16[256,1024]{1,0:T(8,128)(2,1)S(1)}, bf16[256,1024]{1,0:T(8,128)(2,1)}, u32[]{:S(2)}) copy-start(bf16[256,1024]{1,0:T(8,128)(2,1)} %wo_hbm.1) | copy-start | bytes 1572868
  7.3 0.7 %copy-start.6 = (bf16[4,4,256]{2,1,0:T(4,128)(2,1)S(1)}, bf16[4,4,256]{2,1,0:T(4,128)(2,1)}, u32[]{:S(2)}) copy-start(bf16[4,4,256]{2,1,0:T(4,128)(2,1)} %x_hbm.1) | copy-start | bytes 24580
  8.0 0.7 %copy-start.7 = (s32[4,512]{1,0:T(4,128)S(1)}, s32[4,512]{1,0:T(4,128)}, u32[]{:S(2)}) copy-start(s32[4,512]{1,0:T(4,128)} %cvar_hbm.1) | copy-start | bytes 24580
  8.7 0.7 %copy-start.8 = (s32[4,512]{1,0:T(4,128)S(1)}, s32[4,512]{1,0:T(4,128)}, u32[]{:S(2)}) copy-start(s32[4,512]{1,0:T(4,128)} %cmask_hbm.1) | copy-start | bytes 24580
  9.4 0.7 %copy-start.9 = (bf16[1024]{0:T(1024)(128)(2,1)S(1)}, bf16[1024]{0:T(1024)(128)(2,1)}, u32[]{:S(2)}) copy-start(bf16[1024]{0:T(1024)(128)(2,1)} %again_hbm.1) | copy-start | bytes 6148
  10.0 0.7 %copy-start.10 = (bf16[1024]{0:T(1024)(128)(2,1)S(1)}, bf16[1024]{0:T(1024)(128)(2,1)}, u32[]{:S(2)}) copy-start(bf16[1024]{0:T(1024)(128)(2,1)} %fgain_hbm.1) | copy-start | bytes 6148
  10.7 0.7 %copy-start.11 = (s32[4,4]{1,0:T(4,128)S(1)}, s32[4,4]{1,0:T(4,128)}, u32[]{:S(2)}) copy-start(s32[4,4]{1,0:T(4,128)} %nvar_hbm.1) | copy-start | bytes 196
  11.4 0.7 %copy-start.12 = (s32[4,4]{1,0:T(4,128)S(1)}, s32[4,4]{1,0:T(4,128)}, u32[]{:S(2)}) copy-start(s32[4,4]{1,0:T(4,128)} %ntime_hbm.1) | copy-start | bytes 196
  12.1 0.7 %copy-start.13 = (f32[2,16]{1,0:T(2,128)S(1)}, f32[2,16]{1,0:T(2,128)}, u32[]{:S(2)}) copy-start(f32[2,16]{1,0:T(2,128)} %bias_hbm.1) | copy-start | bytes 388
  12.8 0.7 %copy-start.14 = (s32[4]{0:T(128)S(1)}, s32[4]{0:T(128)}, u32[]{:S(2)}) copy-start(s32[4]{0:T(128)} %clen_hbm.1) | copy-start | bytes 52
  13.4 0.7 %copy-start.15 = (s32[4]{0:T(128)S(1)}, s32[4]{0:T(128)}, u32[]{:S(2)}) copy-start(s32[4]{0:T(128)} %fresh_hbm.1) | copy-start | bytes 52
  14.1 0.7 %copy-start.16 = (f32[1,128]{1,0:T(1,128)S(1)}, f32[1,128]{1,0:T(1,128)}, u32[]{:S(2)}) copy-start(f32[1,128]{1,0:T(1,128)} %constant.2.clone.inv_hbm) | copy-start | bytes 1540
